TPU v7x, 32 devices: a whole 2x2x4 slice. The times are simulated.
32 devices in a mesh: group: 1, chan: 32 (over z, y, x, core).
Axes of the slice: x: 2, y: 2, z: 4, core: 2. Of those that a mesh axis runs over, the one named last changes fastest.
Arguments:
- records: bfloat16 [8, 128, 16384], P('group', None, 'chan'), may hold values from -6 to 6
- valid_flags: int32 [8, 128], P('group', 'chan'), may hold values 0 or 1
- source_ids: int32 [64], P('group'), may hold values from 0 to 127, as said below
Outputs:
- correlations: float32 [64, 128, 1001], P('group', 'chan')
Inputs may be any that keep to these rules, and one draw needn't show every extreme that they name: `source_ids`: 64 distinct channel indices.
All inputs are finite; a program needn't handle non-finite values. No bound on the sum of `valid_flags` on one device may be relied on, other than what follows from the above.
Results may differ from a plain program's by a relative error of at most 0.00035.
The roundings to bfloat16 on the way count: a program that leaves them out, or rounds other values in their place, can miss the bound.
Values may be sent and summed in bfloat16 or wider, within the bound.
A program may use at most 64 MiB of HBM per device.

v0:
```python
import math

import jax
import jax.numpy as jnp
import numpy as np
from jax import lax
from jax.experimental import pallas as pl
from jax.experimental.pallas import tpu as pltpu
from jax.sharding import PartitionSpec as P

BAND = 600
HALF_LAG = 500
LAGS = 2 * HALF_LAG + 1
WIDE = 640
LAGS_WIDE = 1024
SPANS = 16
SLOTS = 128
COARSE = 16
STEP = 64

lowest_bin = 8
floor_share = 0.05
epsilon = 1e-06
MESH = pl.DeviceIdType.MESH


def unit(phase, samples, scale=1.0):
    angle = 2.0 * np.pi * (phase % samples) / samples
    return (
        (np.cos(angle) * scale).astype(np.float32),
        (-np.sin(angle) * scale).astype(np.float32),
    )


def forward_parts(samples):
    bins = lowest_bin + np.arange(WIDE, dtype=np.int64)
    keep = (np.arange(WIDE) < BAND).astype(np.float64)
    coarse = np.arange(samples // 4 // STEP, dtype=np.int64) * STEP
    fine = np.arange(STEP, dtype=np.int64)
    sample, column, change = near_ties(samples)
    by_slot = np.zeros((SLOTS, WIDE), np.float32)
    by_slot[:, :SPANS] = column.T
    by_slot[:, SLOTS : SLOTS + SPANS] = change.T
    by_span = np.zeros((SPANS, WIDE), np.float32)
    by_span[:, :SLOTS] = sample
    return np.concatenate(
        (
            *unit(coarse[:, None] * bins[None, :], samples, keep),
            *unit(fine[:, None] * bins[None, :], samples),
            by_slot,
            by_span,
        )
    )


def inverse_parts(samples):
    lags = np.arange(LAGS_WIDE, dtype=np.int64) - HALF_LAG
    coarse = lowest_bin + np.arange(COARSE, dtype=np.int64) * STEP
    fine = np.arange(STEP, dtype=np.int64)
    return np.concatenate(
        (
            *unit(coarse[:, None] * lags[None, :], samples, 1.0 / math.sqrt(BAND)),
            *unit(fine[:, None] * lags[None, :], samples),
        )
    )


def rounded(values):
    return values.astype(np.float32).astype(jnp.bfloat16).astype(np.float32)


def near_ties(samples):
    steps = np.arange(samples)
    single = (steps.astype(np.float32) * np.float32(2.0 * math.pi / samples)).astype(np.float64)
    exact = 2.0 * np.pi * steps / samples
    span = samples // SPANS
    sample = np.full((SPANS, SLOTS), -1, np.int32)
    column = np.full((SPANS, SLOTS), -1, np.int32)
    change = np.zeros((SPANS, SLOTS), np.float32)
    used = np.zeros(SPANS, np.int64)
    phase = np.arange(samples)[:, None] * (lowest_bin + np.arange(BAND))[None, :] % samples
    for wide, (held, folded) in enumerate(
        ((np.cos(single), np.cos(exact)), (-np.sin(single), -np.sin(exact)))
    ):
        difference = rounded(held) - rounded(folded)
        for step in np.nonzero(np.abs(difference) > 1e-6)[0]:
            for n, f in np.argwhere(phase == step):
                g = n // span
                sample[g, used[g]] = n % span
                column[g, used[g]] = wide * WIDE + f
                change[g, used[g]] = difference[step]
                used[g] += 1
    return sample, column, change


def angle_sum(ac, an, bc, bn):
    return ac * bc - an * bn, ac * bn + an * bc


def whiten_rows(acc, ties, flags, rows):
    def part(j, wide):
        return acc[pl.ds(j * rows, rows), pl.ds(wide * WIDE, WIDE)]

    even_r, even_i = part(0, 0) + part(2, 0), part(0, 1) + part(2, 1)
    odd_r, odd_i = part(1, 0) + part(3, 0), part(1, 1) + part(3, 1)
    dif_r, dif_i = part(0, 0) - part(2, 0), part(0, 1) - part(2, 1)
    rot_r, rot_i = part(1, 0) - part(3, 0), part(1, 1) - part(3, 1)
    lane = lax.broadcasted_iota(jnp.int32, (rows, WIDE), 1)
    turn = (lowest_bin + lane) % 4
    real = jnp.where(
        turn == 0,
        even_r + odd_r,
        jnp.where(turn == 1, dif_r + rot_i, jnp.where(turn == 2, even_r - odd_r, dif_r - rot_i)),
    )
    imag = jnp.where(
        turn == 0,
        even_i + odd_i,
        jnp.where(turn == 1, dif_i - rot_r, jnp.where(turn == 2, even_i - odd_i, dif_i + rot_r)),
    )
    real, imag = real + ties[:, :WIDE], imag + ties[:, WIDE:]
    power = real * real + imag * imag
    level = jnp.sum(power, axis=1, keepdims=True) * (1.0 / BAND)
    factor = lax.rsqrt(power + floor_share * level + epsilon)
    weight = flags
    real = jnp.where(lane == BAND, weight, real * factor * weight)
    return real.astype(jnp.bfloat16), (imag * factor * weight).astype(jnp.bfloat16)


def kernel(
    devices, ids_ref, flags_ref, x_ref, forward_hbm, inverse_hbm, out_ref,
    forward, inverse, recv, table, back, acc, pick, put, everyone, held, stacked,
    send_sem, recv_sem, own_sem, part_sem, relay_sem, block_sem,
):
    me = lax.axis_index("chan")
    _, rows, length = x_ref.shape
    sources, ch_local, _ = out_ref.shape
    segments = rows // ch_local
    quarter = devices // 4
    coarse = devices * length // 4 // STEP

    def sending(target, source):
        return pltpu.make_async_remote_copy(
            src_ref=x_ref.at[target],
            dst_ref=recv.at[source],
            send_sem=send_sem,
            recv_sem=recv_sem.at[source],
            device_id={"chan": target},
            device_id_type=MESH,
        )

    parts = (
        pltpu.make_async_copy(forward_hbm, forward, part_sem.at[0]),
        pltpu.make_async_copy(inverse_hbm, inverse, part_sem.at[1]),
        pltpu.make_async_copy(x_ref.at[me], recv.at[me], own_sem),
    )
    for part in parts:
        part.start()
    barrier = pltpu.get_barrier_semaphore()

    @pl.loop(1, devices)
    def _(r):
        pl.semaphore_signal(
            barrier, inc=1, device_id={"chan": (me + r) % devices}, device_id_type=MESH
        )

    pl.semaphore_wait(barrier, devices - 1)

    @pl.loop(1, devices)
    def _(r):
        away = (r + devices // 2 - 2) % (devices - 1) + 1
        sending((me + away) % devices, me).start()

    for part in parts:
        part.wait()

    fine = pl.ds(2 * coarse, STEP), pl.ds(2 * coarse + STEP, STEP)

    @pl.loop(0, coarse)
    def _(a):
        cos, sin = angle_sum(
            forward[pl.ds(a, 1), :],
            forward[pl.ds(coarse + a, 1), :],
            forward[fine[0], :],
            forward[fine[1], :],
        )
        at = pl.ds(pl.multiple_of(a * STEP, STEP), STEP)
        table[at, pl.ds(0, WIDE)] = cos.astype(jnp.bfloat16)
        table[at, pl.ds(WIDE, WIDE)] = sin.astype(jnp.bfloat16)

    span = devices * length // SPANS
    by_slot = 2 * coarse + 2 * STEP
    for g in range(SPANS):
        sample = forward[pl.ds(by_slot + SLOTS + g, 1), pl.ds(0, SLOTS)].astype(jnp.int32)
        here = lax.broadcasted_iota(jnp.int32, (span, SLOTS), 0) == sample
        pick[g] = jnp.where(here, 1.0, 0.0).astype(jnp.bfloat16)
        column = forward[pl.ds(by_slot, SLOTS), pl.ds(g, 1)].astype(jnp.int32)
        change = forward[pl.ds(by_slot, SLOTS), pl.ds(SLOTS + g, 1)]
        there = lax.broadcasted_iota(jnp.int32, (SLOTS, 2 * WIDE), 1) == column
        put[pl.ds(g * SLOTS, SLOTS), :] = jnp.where(there, change, 0.0).astype(jnp.bfloat16)

    for a in range(WIDE // STEP):
        cos, sin = angle_sum(
            inverse[pl.ds(a, 1), :],
            inverse[pl.ds(COARSE + a, 1), :],
            inverse[pl.ds(2 * COARSE, STEP), :],
            inverse[pl.ds(2 * COARSE + STEP, STEP), :],
        )
        back[pl.ds(a * STEP, STEP), :] = cos.astype(jnp.bfloat16)
        back[pl.ds(WIDE + a * STEP, STEP), :] = sin.astype(jnp.bfloat16)

    acc[...] = jnp.zeros_like(acc)

    @pl.loop(0, quarter)
    def _(i):
        for j in range(4):
            source = i + j * quarter

            @pl.when(source != me)
            def _():
                sending(source, source).wait_recv()

        piece = jnp.concatenate([recv[i + j * quarter] for j in range(4)], axis=0)
        acc[...] += jnp.dot(
            piece,
            table[pl.ds(pl.multiple_of(i * length, length), length), :],
            preferred_element_type=jnp.float32,
        )

    per = devices // SPANS
    picked = []
    for g in range(SPANS):
        piece = jnp.concatenate([recv[g * per + t] for t in range(per)], axis=1)
        picked.append(
            jnp.dot(piece, pick[g], preferred_element_type=jnp.float32).astype(jnp.bfloat16)
        )
    ties = jnp.dot(
        jnp.concatenate(picked, axis=1), put[...], preferred_element_type=jnp.float32
    )

    square = (segments, segments)
    diagonal = lax.broadcasted_iota(jnp.int32, square, 0) == lax.broadcasted_iota(
        jnp.int32, square, 1
    )
    flags = flags_ref[...].astype(jnp.float32)
    flags = jnp.concatenate(
        [
            jnp.sum(jnp.where(diagonal, flags[c : c + 1, :], 0.0), axis=1, keepdims=True)
            for c in range(ch_local)
        ],
        axis=0,
    )
    real, imag = whiten_rows(acc, ties, flags, rows)
    own_rows = pl.ds(me * ch_local, ch_local)
    everyone[own_rows, :, pl.ds(0, WIDE)] = real.reshape(ch_local, segments, WIDE)
    everyone[own_rows, :, pl.ds(WIDE, WIDE)] = imag.reshape(ch_local, segments, WIDE)

    depth = devices // 8
    z = me // 8
    flip = {bit: me + bit - 2 * bit * (me // bit % 2) for bit in (1, 2, 4)}

    def relay(source, h, target):
        block = everyone.at[source * ch_local + h]
        return pltpu.make_async_remote_copy(
            src_ref=block,
            dst_ref=block,
            send_sem=relay_sem,
            recv_sem=block_sem.at[source, h],
            device_id={"chan": target},
            device_id_type=MESH,
        )

    def each_relay(zs, far, h, act):
        first, second = ((4, 2), (2, 4))[h % 2]
        base = (me, flip[first], flip[second], flip[first] + flip[second] - me)[far]
        source = base + (zs - z) * 8
        if far == 0:

            @pl.when((zs <= z) & (z + 1 < depth))
            def _():
                act(relay(source, h, me + 8))

            @pl.when((zs >= z) & (z > 0))
            def _():
                act(relay(source, h, me - 8))

            act(relay(source, h, flip[first]))
        if far <= 1:
            act(relay(source, h, flip[second]))
        act(relay(source, h, flip[1]))

    def each_block(act):
        @pl.loop(0, depth + 2)
        def _(wave):
            for far, hops in enumerate((0, 1, 1, 2)):
                k = wave - hops
                for side in (-1, 1):
                    zs = z + side * k
                    real_block = (k >= 0) & (k < depth) & (zs >= 0) & (zs < depth)
                    if side == 1:
                        real_block = real_block & (k > 0)

                    @pl.when(real_block)
                    def _():
                        for h in range(ch_local):
                            act(zs, far, h)

    def forward_block(zs, far, h):
        first, second = ((4, 2), (2, 4))[h % 2]
        base = (me, flip[first], flip[second], flip[first] + flip[second] - me)[far]
        source = base + (zs - z) * 8

        @pl.when(source != me)
        def _():
            relay(source, h, me).wait_recv()

        each_relay(zs, far, h, lambda copy: copy.start())

    each_block(forward_block)

    @pl.loop(0, devices // 2)
    def _(r):
        source = 2 * r + flip[1] % 2
        for h in range(ch_local):
            relay(source, h, me).wait_recv()

    group = 8

    @pl.loop(0, sources // group)
    def _(block):
        for s in range(group):
            held[s] = everyone[ids_ref[block * group + s]].astype(jnp.float32)
        lane = lax.broadcasted_iota(jnp.int32, (group, WIDE), 1)
        src_r, src_i = held[:, :, pl.ds(0, WIDE)], held[:, :, pl.ds(WIDE, WIDE)]
        for c in range(ch_local):
            mine = everyone[me * ch_local + c].astype(jnp.float32)
            rec_r, rec_i = mine[None, :, :WIDE], mine[None, :, WIDE:]
            real = jnp.sum(src_r * rec_r + src_i * rec_i, axis=1)
            imag = jnp.sum(src_i * rec_r - src_r * rec_i, axis=1)
            counts = jnp.sum(jnp.where(lane == BAND, real, 0.0), axis=1, keepdims=True)
            divisor = jnp.maximum(counts, 1.0)
            at = pl.ds(pl.multiple_of(block * group, group), group)
            stacked[c, at, pl.ds(0, WIDE)] = jnp.where(lane < BAND, real / divisor, 0.0)
            stacked[c, at, pl.ds(WIDE, WIDE)] = imag / divisor

    for c in range(ch_local):
        lags = jnp.dot(
            stacked[c].astype(jnp.bfloat16), back[...], preferred_element_type=jnp.float32
        )
        out_ref[:, c, :] = lags[:, :LAGS]

    @pl.loop(1, devices)
    def _(r):
        sending((me + r) % devices, me).wait_send()

    each_block(lambda zs, far, h: each_relay(zs, far, h, lambda copy: copy.wait_send()))


def per_device(records, valid_flags, source_ids):
    devices = lax.axis_size("chan")
    segments, channels, length = records.shape
    ch_local = channels // devices
    rows = ch_local * segments
    samples = length * devices
    sources = source_ids.shape[0]
    x = records.reshape(segments, devices, ch_local, length).transpose(1, 2, 0, 3)
    x = x.reshape(devices, rows, length)
    forward, inverse = forward_parts(samples), inverse_parts(samples)
    vmem = pl.BlockSpec(memory_space=pltpu.VMEM)
    anywhere = pl.BlockSpec(memory_space=pl.ANY)
    return pl.pallas_call(
        lambda *refs: kernel(devices, *refs),
        out_shape=jax.ShapeDtypeStruct((sources, ch_local, LAGS), jnp.float32),
        in_specs=[pl.BlockSpec(memory_space=pltpu.SMEM), vmem, vmem, anywhere, anywhere],
        out_specs=vmem,
        scratch_shapes=[
            pltpu.VMEM(forward.shape, jnp.float32),
            pltpu.VMEM(inverse.shape, jnp.float32),
            pltpu.VMEM(x.shape, jnp.bfloat16),
            pltpu.VMEM((samples // 4, 2 * WIDE), jnp.bfloat16),
            pltpu.VMEM((2 * WIDE, LAGS_WIDE), jnp.bfloat16),
            pltpu.VMEM((4 * rows, 2 * WIDE), jnp.float32),
            pltpu.VMEM((SPANS, samples // SPANS, SLOTS), jnp.bfloat16),
            pltpu.VMEM((SPANS * SLOTS, 2 * WIDE), jnp.bfloat16),
            pltpu.VMEM((channels, segments, 2 * WIDE), jnp.bfloat16),
            pltpu.VMEM((8, segments, 2 * WIDE), jnp.float32),
            pltpu.VMEM((ch_local, sources, 2 * WIDE), jnp.float32),
            pltpu.SemaphoreType.DMA,
            pltpu.SemaphoreType.DMA((devices,)),
            pltpu.SemaphoreType.DMA,
            pltpu.SemaphoreType.DMA((2,)),
            pltpu.SemaphoreType.DMA,
            pltpu.SemaphoreType.DMA((devices, ch_local)),
        ],
        compiler_params=pltpu.CompilerParams(
            collective_id=0, has_side_effects=True, vmem_limit_bytes=56 << 20
        ),
        name="correlate",
    )(source_ids, valid_flags.T, x, jnp.asarray(forward), jnp.asarray(inverse))


def solution(mesh):
    return jax.shard_map(
        per_device,
        mesh=mesh,
        in_specs=(P("group", None, "chan"), P("group", "chan"), P("group")),
        out_specs=P("group", "chan", None),
        check_vma=False,
    )
```

profile of v0, /device:TPU:1, one launch (start us, length us, event | category | flops | bytes accessed | tf_op | source)
XLA Modules:
  0.0 67.8 jit_solution(5944200795703947597)
XLA Ops:
  0.0 2.8 %copy.7 = bf16[8,128,512]{2,0,1:T(8,128)(2,1)} copy(bf16[8,128,512]{2,1,0:T(8,128)(2,1)} %param.5) | data formatting | bytes 2097152 | tf_op jit(solution)/shard_map/reshape | solution.py:365
  2.8 62.8 %correlate.1 = f32[64,4,1001]{2,1,0:T(4,128)} custom-call(s32[64]{0:T(128)} %refs_0_.1, s32[4,8]{1,0:T(4,128)} %bitcast.7, bf16[32,32,512]{2,1,0:T(8,128)(2,1)} %bitcast.6, f32[400,640]{1,0:T(8,128)} %constant.4.clone.refs_3_, f32[160,1024]{1,0:T(8,128)} %constant.5.clone.refs_4_), custom_call_target="tpu_custom_call" | custom-call | tf_op jit(solution)/shard_map/correlate/pallas_call | solution.py:370
  65.6 2.3 %copy.9 = f32[64,4,1001]{2,1,0:T(4,128)} copy(f32[64,4,1001]{2,1,0:T(4,128)} %correlate.1) | data formatting | bytes 2050048
where the time goes:
time: 68 us; the launch traced here: 67.8 us
  Pallas kernels  62.8 us (92%)
  local copies, waits for them, and re-layouts  5.04 us (7%)
    pallas_call x1, Pallas kernels, per_device(): pl.pallas_call(lambda *refs: kernel(devices, *refs), out_shape=jax.ShapeD...  62.8 us
    reshape x1, local copies, waits for them, and re-layouts, per_device(): records.reshape(segments, devices, ch_local, length).transpose(1, 2, 0, 3)  2.77 us
    unnamed x1, local copies, waits for them, and re-layouts  2.26 us

commit v1 on v0

--- a/solution.py
+++ b/solution.py
@@ -17,6 +17,8 @@
 SLOTS = 128
 COARSE = 16
 STEP = 64
+LAG_TILE = 256
+LANES = 128
 
 lowest_bin = 8
 floor_share = 0.05
@@ -97,27 +99,22 @@
     return ac * bc - an * bn, ac * bn + an * bc
 
 
-def whiten_rows(acc, ties, flags, rows):
+def turned(acc, rows, half):
     def part(j, wide):
         return acc[pl.ds(j * rows, rows), pl.ds(wide * WIDE, WIDE)]
 
-    even_r, even_i = part(0, 0) + part(2, 0), part(0, 1) + part(2, 1)
-    odd_r, odd_i = part(1, 0) + part(3, 0), part(1, 1) + part(3, 1)
-    dif_r, dif_i = part(0, 0) - part(2, 0), part(0, 1) - part(2, 1)
-    rot_r, rot_i = part(1, 0) - part(3, 0), part(1, 1) - part(3, 1)
-    lane = lax.broadcasted_iota(jnp.int32, (rows, WIDE), 1)
-    turn = (lowest_bin + lane) % 4
-    real = jnp.where(
-        turn == 0,
-        even_r + odd_r,
-        jnp.where(turn == 1, dif_r + rot_i, jnp.where(turn == 2, even_r - odd_r, dif_r - rot_i)),
-    )
-    imag = jnp.where(
-        turn == 0,
-        even_i + odd_i,
-        jnp.where(turn == 1, dif_i - rot_r, jnp.where(turn == 2, even_i - odd_i, dif_i + rot_r)),
-    )
-    real, imag = real + ties[:, :WIDE], imag + ties[:, WIDE:]
+    (low_r, low_i), (high_r, high_i) = ((part(j, 0), part(j, 1)) for j in (0, 1))
+    turn = (lowest_bin + lax.broadcasted_iota(jnp.int32, (rows, WIDE), 1)) % 4
+    swap_r = jnp.where(turn % 2 == 0, high_r, high_i)
+    swap_i = jnp.where(turn % 2 == 0, high_i, -high_r)
+    real = low_r + jnp.where(turn < 2, swap_r, -swap_r)
+    imag = low_i + jnp.where(turn < 2, swap_i, -swap_i)
+    flip = (half == 1) & (turn % 2 == 1)
+    return jnp.where(flip, -real, real), jnp.where(flip, -imag, imag)
+
+
+def whiten_rows(real, imag, flags):
+    lane = lax.broadcasted_iota(jnp.int32, real.shape, 1)
     power = real * real + imag * imag
     level = jnp.sum(power, axis=1, keepdims=True) * (1.0 / BAND)
     factor = lax.rsqrt(power + floor_share * level + epsilon)
@@ -127,48 +124,85 @@
 
 
 def kernel(
-    devices, ids_ref, flags_ref, x_ref, forward_hbm, inverse_hbm, out_ref,
-    forward, inverse, recv, table, back, acc, pick, put, everyone, held, stacked,
-    send_sem, recv_sem, own_sem, part_sem, relay_sem, block_sem,
+    devices, ids_ref, flags_ref, x_hbm, forward_hbm, inverse_hbm, out_ref,
+    forward, inverse, recv, table, back, acc, pick, put, whole, share, halves,
+    everyone, held, stacked,
+    send_sem, recv_sem, own_sem, part_sem, share_sem, half_sem, relay_sem, block_sem,
 ):
     me = lax.axis_index("chan")
-    _, rows, length = x_ref.shape
+    half, segments, tile, length = recv.shape
     sources, ch_local, _ = out_ref.shape
-    segments = rows // ch_local
+    rows = segments * tile
     quarter = devices // 4
+    chips = half // 2
     coarse = devices * length // 4 // STEP
+    side, seat = me // half, me % half
+    chip, core = seat // 2, me % 2
+    received = recv.reshape(half, rows, length)
+
+    def channels_of(target):
+        start = ch_local * (target % 2 * half + target // 2 * 2)
+        return x_hbm.at[:, pl.ds(pl.multiple_of(start, tile), tile), :]
 
     def sending(target, source):
         return pltpu.make_async_remote_copy(
-            src_ref=x_ref.at[target],
+            src_ref=channels_of(target),
             dst_ref=recv.at[source],
             send_sem=send_sem,
             recv_sem=recv_sem.at[source],
-            device_id={"chan": target},
+            device_id={"chan": side * half + target},
             device_id_type=MESH,
         )
 
     parts = (
         pltpu.make_async_copy(forward_hbm, forward, part_sem.at[0]),
         pltpu.make_async_copy(inverse_hbm, inverse, part_sem.at[1]),
-        pltpu.make_async_copy(x_ref.at[me], recv.at[me], own_sem),
+        pltpu.make_async_copy(channels_of(seat), recv.at[seat], own_sem),
     )
     for part in parts:
         part.start()
     barrier = pltpu.get_barrier_semaphore()
-
-    @pl.loop(1, devices)
+    depth = devices // 8
+    z = me // 8
+    across = (1 - side) * half + 2 * chip
+
+    def greet(device):
+        pl.semaphore_signal(barrier, inc=1, device_id={"chan": device}, device_id_type=MESH)
+
+    greet(across)
+    greet(across + 1)
+
+    @pl.when(z == depth // 2 - 1)
+    def _():
+        greet(me + 8)
+
+    @pl.when(z == depth // 2)
+    def _():
+        greet(me - 8)
+
+    @pl.loop(1, half)
     def _(r):
-        pl.semaphore_signal(
-            barrier, inc=1, device_id={"chan": (me + r) % devices}, device_id_type=MESH
-        )
-
-    pl.semaphore_wait(barrier, devices - 1)
-
-    @pl.loop(1, devices)
-    def _(r):
-        away = (r + devices // 2 - 2) % (devices - 1) + 1
-        sending((me + away) % devices, me).start()
+        greet(side * half + (seat + r) % half)
+
+    middle = (z == depth // 2 - 1) | (z == depth // 2)
+
+    @pl.when(middle)
+    def _():
+        pl.semaphore_wait(barrier, half + 2)
+
+    @pl.when(jnp.logical_not(middle))
+    def _():
+        pl.semaphore_wait(barrier, half + 1)
+
+    for role in (1 - side, side):
+
+        @pl.loop(0, chips)
+        def _(k):
+            target = 2 * ((chip + chips // 2 + k) % chips) + role
+
+            @pl.when(target != seat)
+            def _():
+                sending(target, seat).start()
 
     for part in parts:
         part.wait()
@@ -188,13 +222,22 @@
         table[at, pl.ds(WIDE, WIDE)] = sin.astype(jnp.bfloat16)
 
     span = devices * length // SPANS
+    spans = SPANS // 2
     by_slot = 2 * coarse + 2 * STEP
-    for g in range(SPANS):
-        sample = forward[pl.ds(by_slot + SLOTS + g, 1), pl.ds(0, SLOTS)].astype(jnp.int32)
+    for g in range(spans):
+        by_side = [
+            forward[pl.ds(by_slot + SLOTS + first + g, 1), pl.ds(0, SLOTS)]
+            for first in (0, spans)
+        ]
+        sample = jnp.where(side == 0, by_side[0], by_side[1]).astype(jnp.int32)
         here = lax.broadcasted_iota(jnp.int32, (span, SLOTS), 0) == sample
         pick[g] = jnp.where(here, 1.0, 0.0).astype(jnp.bfloat16)
-        column = forward[pl.ds(by_slot, SLOTS), pl.ds(g, 1)].astype(jnp.int32)
-        change = forward[pl.ds(by_slot, SLOTS), pl.ds(SLOTS + g, 1)]
+        by_side = [
+            forward[pl.ds(by_slot, SLOTS), pl.ds(first + g, 1)]
+            for first in (0, spans, SLOTS, SLOTS + spans)
+        ]
+        column = jnp.where(side == 0, by_side[0], by_side[1]).astype(jnp.int32)
+        change = jnp.where(side == 0, by_side[2], by_side[3])
         there = lax.broadcasted_iota(jnp.int32, (SLOTS, 2 * WIDE), 1) == column
         put[pl.ds(g * SLOTS, SLOTS), :] = jnp.where(there, change, 0.0).astype(jnp.bfloat16)
 
@@ -212,14 +255,14 @@
 
     @pl.loop(0, quarter)
     def _(i):
-        for j in range(4):
+        for j in range(2):
             source = i + j * quarter
 
-            @pl.when(source != me)
+            @pl.when(source != seat)
             def _():
                 sending(source, source).wait_recv()
 
-        piece = jnp.concatenate([recv[i + j * quarter] for j in range(4)], axis=0)
+        piece = jnp.concatenate([received[i], received[i + quarter]], axis=0)
         acc[...] += jnp.dot(
             piece,
             table[pl.ds(pl.multiple_of(i * length, length), length), :],
@@ -228,14 +271,56 @@
 
     per = devices // SPANS
     picked = []
-    for g in range(SPANS):
-        piece = jnp.concatenate([recv[g * per + t] for t in range(per)], axis=1)
+    for g in range(spans):
+        piece = jnp.concatenate([received[g * per + t] for t in range(per)], axis=1)
         picked.append(
             jnp.dot(piece, pick[g], preferred_element_type=jnp.float32).astype(jnp.bfloat16)
         )
     ties = jnp.dot(
         jnp.concatenate(picked, axis=1), put[...], preferred_element_type=jnp.float32
     )
+    real, imag = turned(acc, rows, side)
+    for k in range(2 * WIDE // LANES):
+        at = k * LANES
+        source = real[:, at : at + LANES] if at < WIDE else imag[:, at - WIDE : at - WIDE + LANES]
+        whole[k] = source + ties[:, at : at + LANES]
+    for c in range(tile):
+        for k in range(2 * WIDE // LANES):
+            share[c, :, pl.ds(k * LANES, LANES)] = whole[k, pl.ds(c, segments, stride=tile), :]
+
+    def sharing(target, k):
+        return pltpu.make_async_remote_copy(
+            src_ref=share.at[pl.ds(k * ch_local, ch_local)],
+            dst_ref=halves.at[side],
+            send_sem=share_sem,
+            recv_sem=half_sem.at[side],
+            device_id={"chan": target},
+            device_id_type=MESH,
+        )
+
+    def arriving(from_side):
+        return pltpu.make_async_remote_copy(
+            src_ref=share.at[pl.ds(0, ch_local)],
+            dst_ref=halves.at[from_side],
+            send_sem=share_sem,
+            recv_sem=half_sem.at[from_side],
+            device_id={"chan": across},
+            device_id_type=MESH,
+        )
+
+    @pl.when(core == side)
+    def _():
+        sharing(me + 1 - 2 * core, 1 - core).start()
+        for c in range(ch_local):
+            halves[side, c] = share[core * ch_local + c]
+
+    @pl.when(core != side)
+    def _():
+        sharing(across, 0).start()
+        sharing(across + 1, 1).start()
+        arriving(side).wait_recv()
+
+    arriving(1 - side).wait_recv()
 
     square = (segments, segments)
     diagonal = lax.broadcasted_iota(jnp.int32, square, 0) == lax.broadcasted_iota(
@@ -249,13 +334,12 @@
         ],
         axis=0,
     )
-    real, imag = whiten_rows(acc, ties, flags, rows)
+    total = (halves[0] + halves[1]).reshape(ch_local * segments, 2 * WIDE)
+    real, imag = whiten_rows(total[:, :WIDE], total[:, WIDE:], flags)
     own_rows = pl.ds(me * ch_local, ch_local)
     everyone[own_rows, :, pl.ds(0, WIDE)] = real.reshape(ch_local, segments, WIDE)
     everyone[own_rows, :, pl.ds(WIDE, WIDE)] = imag.reshape(ch_local, segments, WIDE)
 
-    depth = devices // 8
-    z = me // 8
     flip = {bit: me + bit - 2 * bit * (me // bit % 2) for bit in (1, 2, 4)}
 
     def relay(source, h, target):
@@ -338,19 +422,39 @@
             imag = jnp.sum(src_i * rec_r - src_r * rec_i, axis=1)
             counts = jnp.sum(jnp.where(lane == BAND, real, 0.0), axis=1, keepdims=True)
             divisor = jnp.maximum(counts, 1.0)
-            at = pl.ds(pl.multiple_of(block * group, group), group)
-            stacked[c, at, pl.ds(0, WIDE)] = jnp.where(lane < BAND, real / divisor, 0.0)
-            stacked[c, at, pl.ds(WIDE, WIDE)] = imag / divisor
-
-    for c in range(ch_local):
+            at = pl.ds(block * (group * ch_local) + c, group, stride=ch_local)
+            real = jnp.where(lane < BAND, real / divisor, 0.0)
+            imag = imag / divisor
+            for k in range(WIDE // LANES):
+                stacked[k, at, :] = real[:, k * LANES : (k + 1) * LANES]
+                stacked[WIDE // LANES + k, at, :] = imag[:, k * LANES : (k + 1) * LANES]
+
+    left = jnp.concatenate(
+        [stacked[k].astype(jnp.bfloat16) for k in range(2 * WIDE // LANES)], axis=1
+    )
+    for first in range(0, LAGS, LAG_TILE):
         lags = jnp.dot(
-            stacked[c].astype(jnp.bfloat16), back[...], preferred_element_type=jnp.float32
-        )
-        out_ref[:, c, :] = lags[:, :LAGS]
-
-    @pl.loop(1, devices)
-    def _(r):
-        sending((me + r) % devices, me).wait_send()
+            left, back[:, pl.ds(first, LAG_TILE)], preferred_element_type=jnp.float32
+        )
+        lags = lags.reshape(sources, ch_local, LAG_TILE)
+        width = min(LAG_TILE, LAGS - first)
+        out_ref[:, :, pl.ds(first, width)] = lags[:, :, :width]
+
+    for role in (1 - side, side):
+
+        @pl.loop(0, chips)
+        def _(k):
+            target = 2 * ((chip + k) % chips) + role
+
+            @pl.when(target != seat)
+            def _():
+                sending(target, seat).wait_send()
+
+    sharing(me + 1 - 2 * core, 1 - core).wait_send()
+
+    @pl.when(core != side)
+    def _():
+        sharing(across, 0).wait_send()
 
     each_block(lambda zs, far, h: each_relay(zs, far, h, lambda copy: copy.wait_send()))
 
@@ -362,30 +466,33 @@
     rows = ch_local * segments
     samples = length * devices
     sources = source_ids.shape[0]
-    x = records.reshape(segments, devices, ch_local, length).transpose(1, 2, 0, 3)
-    x = x.reshape(devices, rows, length)
     forward, inverse = forward_parts(samples), inverse_parts(samples)
     vmem = pl.BlockSpec(memory_space=pltpu.VMEM)
     anywhere = pl.BlockSpec(memory_space=pl.ANY)
     return pl.pallas_call(
         lambda *refs: kernel(devices, *refs),
         out_shape=jax.ShapeDtypeStruct((sources, ch_local, LAGS), jnp.float32),
-        in_specs=[pl.BlockSpec(memory_space=pltpu.SMEM), vmem, vmem, anywhere, anywhere],
+        in_specs=[pl.BlockSpec(memory_space=pltpu.SMEM), vmem, anywhere, anywhere, anywhere],
         out_specs=vmem,
         scratch_shapes=[
             pltpu.VMEM(forward.shape, jnp.float32),
             pltpu.VMEM(inverse.shape, jnp.float32),
-            pltpu.VMEM(x.shape, jnp.bfloat16),
+            pltpu.VMEM((devices // 2, segments, 2 * ch_local, length), jnp.bfloat16),
             pltpu.VMEM((samples // 4, 2 * WIDE), jnp.bfloat16),
             pltpu.VMEM((2 * WIDE, LAGS_WIDE), jnp.bfloat16),
             pltpu.VMEM((4 * rows, 2 * WIDE), jnp.float32),
-            pltpu.VMEM((SPANS, samples // SPANS, SLOTS), jnp.bfloat16),
-            pltpu.VMEM((SPANS * SLOTS, 2 * WIDE), jnp.bfloat16),
+            pltpu.VMEM((SPANS // 2, samples // SPANS, SLOTS), jnp.bfloat16),
+            pltpu.VMEM((SPANS // 2 * SLOTS, 2 * WIDE), jnp.bfloat16),
+            pltpu.VMEM((2 * WIDE // LANES, 2 * rows, LANES), jnp.float32),
+            pltpu.VMEM((2 * ch_local, segments, 2 * WIDE), jnp.float32),
+            pltpu.VMEM((2, ch_local, segments, 2 * WIDE), jnp.float32),
             pltpu.VMEM((channels, segments, 2 * WIDE), jnp.bfloat16),
             pltpu.VMEM((8, segments, 2 * WIDE), jnp.float32),
-            pltpu.VMEM((ch_local, sources, 2 * WIDE), jnp.float32),
+            pltpu.VMEM((2 * WIDE // LANES, ch_local * sources, LANES), jnp.float32),
             pltpu.SemaphoreType.DMA,
-            pltpu.SemaphoreType.DMA((devices,)),
+            pltpu.SemaphoreType.DMA((devices // 2,)),
+            pltpu.SemaphoreType.DMA,
+            pltpu.SemaphoreType.DMA((2,)),
             pltpu.SemaphoreType.DMA,
             pltpu.SemaphoreType.DMA((2,)),
             pltpu.SemaphoreType.DMA,
@@ -395,7 +502,7 @@
             collective_id=0, has_side_effects=True, vmem_limit_bytes=56 << 20
         ),
         name="correlate",
-    )(source_ids, valid_flags.T, x, jnp.asarray(forward), jnp.asarray(inverse))
+    )(source_ids, valid_flags.T, records, jnp.asarray(forward), jnp.asarray(inverse))
 
 
 def solution(mesh):

time: 68 us -> 55.5 us (0.82)
  Pallas kernels: 62.8 us -> 53.1 us
  local copies, waits for them, and re-layouts: 5.04 us -> 2.26 us
    pallas_call x1, Pallas kernels: 62.8 us -> 53.1 us  [per_device(): pl.pallas_call(lambda *refs: kernel(devices, *refs), out_shape=jax.ShapeD...]
    reshape x1 -> x0, local copies, waits for them, and re-layouts: 2.77 us -> none  [per_device(): records.reshape(segments, devices, ch_local, length).transpose(1, 2, 0, 3)]
where the time goes in v1:
time: 55.5 us; the launch traced here: 55.4 us
  Pallas kernels  53.1 us (96%)
  local copies, waits for them, and re-layouts  2.26 us (4%)
    pallas_call x1, Pallas kernels, per_device(): pl.pallas_call(lambda *refs: kernel(devices, *refs), out_shape=jax.ShapeD...  53.1 us
    unnamed x1, local copies, waits for them, and re-layouts  2.26 us

profile of v1, /device:TPU:1, one launch (start us, length us, event | category | flops | bytes accessed | tf_op | source)
XLA Modules:
  0.0 55.4 jit_solution(2393754842865646981)
XLA Ops:
  0.0 53.1 %correlate.1 = f32[64,4,1001]{2,1,0:T(4,128)} custom-call(s32[64]{0:T(128)} %refs_0_.1, s32[4,8]{1,0:T(4,128)} %bitcast.1, bf16[8,128,512]{2,1,0:T(8,128)(2,1)} %refs_2_.1, f32[400,640]{1,0:T(8,128)} %constant.4.clone.refs_3_, f32[160,1024]{1,0:T(8,128)} %constant.5.clone.refs_4_), custom_call_target="tpu_custom_call" | custom-call | tf_op jit(solution)/shard_map/correlate/pallas_call | solution.py:472
  53.1 2.3 %copy.7 = f32[64,4,1001]{2,1,0:T(4,128)} copy(f32[64,4,1001]{2,1,0:T(4,128)} %correlate.1) | data formatting | bytes 2050048

commit v2 on v1

--- a/solution.py
+++ b/solution.py
@@ -19,6 +19,8 @@
 STEP = 64
 LAG_TILE = 256
 LANES = 128
+PARTS = 2
+PAIR = 2
 
 lowest_bin = 8
 floor_share = 0.05
@@ -126,11 +128,11 @@
 def kernel(
     devices, ids_ref, flags_ref, x_hbm, forward_hbm, inverse_hbm, out_ref,
     forward, inverse, recv, table, back, acc, pick, put, whole, share, halves,
-    everyone, held, stacked,
+    everyone, held, mine, stacked,
     send_sem, recv_sem, own_sem, part_sem, share_sem, half_sem, relay_sem, block_sem,
 ):
     me = lax.axis_index("chan")
-    half, segments, tile, length = recv.shape
+    _, half, segments, tile, length = recv.shape
     sources, ch_local, _ = out_ref.shape
     rows = segments * tile
     quarter = devices // 4
@@ -138,18 +140,18 @@
     coarse = devices * length // 4 // STEP
     side, seat = me // half, me % half
     chip, core = seat // 2, me % 2
-    received = recv.reshape(half, rows, length)
-
-    def channels_of(target):
-        start = ch_local * (target % 2 * half + target // 2 * 2)
-        return x_hbm.at[:, pl.ds(pl.multiple_of(start, tile), tile), :]
-
-    def sending(target, source):
+    received = recv.reshape(PARTS, half, rows, length)
+
+    def channels_of(part, target):
+        start = pl.multiple_of(ch_local * (target % 2 * half + target // 2 * 2), tile)
+        return x_hbm.at[pl.ds(part * segments, segments), pl.ds(start, tile), :]
+
+    def sending(part, target, source):
         return pltpu.make_async_remote_copy(
-            src_ref=channels_of(target),
-            dst_ref=recv.at[source],
+            src_ref=channels_of(part, target),
+            dst_ref=recv.at[part, source],
             send_sem=send_sem,
-            recv_sem=recv_sem.at[source],
+            recv_sem=recv_sem.at[part, source],
             device_id={"chan": side * half + target},
             device_id_type=MESH,
         )
@@ -157,10 +159,11 @@
     parts = (
         pltpu.make_async_copy(forward_hbm, forward, part_sem.at[0]),
         pltpu.make_async_copy(inverse_hbm, inverse, part_sem.at[1]),
-        pltpu.make_async_copy(channels_of(seat), recv.at[seat], own_sem),
-    )
-    for part in parts:
-        part.start()
+        pltpu.make_async_copy(channels_of(0, seat), recv.at[0, seat], own_sem.at[0]),
+        pltpu.make_async_copy(channels_of(1, seat), recv.at[1, seat], own_sem.at[1]),
+    )
+    for copy in parts:
+        copy.start()
     barrier = pltpu.get_barrier_semaphore()
     depth = devices // 8
     z = me // 8
@@ -194,18 +197,22 @@
     def _():
         pl.semaphore_wait(barrier, half + 1)
 
-    for role in (1 - side, side):
-
-        @pl.loop(0, chips)
-        def _(k):
-            target = 2 * ((chip + chips // 2 + k) % chips) + role
-
-            @pl.when(target != seat)
-            def _():
-                sending(target, seat).start()
-
-    for part in parts:
-        part.wait()
+    def each_sending(act):
+        for part in range(PARTS):
+            for role in (1 - side, side):
+
+                @pl.loop(0, chips)
+                def _(k):
+                    target = 2 * ((chip + chips // 2 + k) % chips) + role
+
+                    @pl.when(target != seat)
+                    def _():
+                        act(sending(part, target, seat))
+
+    each_sending(lambda copy: copy.start())
+
+    for copy in parts:
+        copy.wait()
 
     fine = pl.ds(2 * coarse, STEP), pl.ds(2 * coarse + STEP, STEP)
 
@@ -251,173 +258,197 @@
         back[pl.ds(a * STEP, STEP), :] = cos.astype(jnp.bfloat16)
         back[pl.ds(WIDE + a * STEP, STEP), :] = sin.astype(jnp.bfloat16)
 
-    acc[...] = jnp.zeros_like(acc)
-
-    @pl.loop(0, quarter)
-    def _(i):
-        for j in range(2):
-            source = i + j * quarter
-
-            @pl.when(source != seat)
-            def _():
-                sending(source, source).wait_recv()
-
-        piece = jnp.concatenate([received[i], received[i + quarter]], axis=0)
-        acc[...] += jnp.dot(
-            piece,
-            table[pl.ds(pl.multiple_of(i * length, length), length), :],
-            preferred_element_type=jnp.float32,
-        )
-
     per = devices // SPANS
-    picked = []
-    for g in range(spans):
-        piece = jnp.concatenate([received[g * per + t] for t in range(per)], axis=1)
-        picked.append(
-            jnp.dot(piece, pick[g], preferred_element_type=jnp.float32).astype(jnp.bfloat16)
-        )
-    ties = jnp.dot(
-        jnp.concatenate(picked, axis=1), put[...], preferred_element_type=jnp.float32
-    )
-    real, imag = turned(acc, rows, side)
-    for k in range(2 * WIDE // LANES):
-        at = k * LANES
-        source = real[:, at : at + LANES] if at < WIDE else imag[:, at - WIDE : at - WIDE + LANES]
-        whole[k] = source + ties[:, at : at + LANES]
-    for c in range(tile):
-        for k in range(2 * WIDE // LANES):
-            share[c, :, pl.ds(k * LANES, LANES)] = whole[k, pl.ds(c, segments, stride=tile), :]
-
-    def sharing(target, k):
+
+    def sharing(part, target, k):
         return pltpu.make_async_remote_copy(
-            src_ref=share.at[pl.ds(k * ch_local, ch_local)],
-            dst_ref=halves.at[side],
+            src_ref=share.at[part, pl.ds(k * ch_local, ch_local)],
+            dst_ref=halves.at[part, side],
             send_sem=share_sem,
-            recv_sem=half_sem.at[side],
+            recv_sem=half_sem.at[part, side],
             device_id={"chan": target},
             device_id_type=MESH,
         )
 
-    def arriving(from_side):
+    def arriving(part, from_side):
         return pltpu.make_async_remote_copy(
-            src_ref=share.at[pl.ds(0, ch_local)],
-            dst_ref=halves.at[from_side],
+            src_ref=share.at[part, pl.ds(0, ch_local)],
+            dst_ref=halves.at[part, from_side],
             send_sem=share_sem,
-            recv_sem=half_sem.at[from_side],
+            recv_sem=half_sem.at[part, from_side],
             device_id={"chan": across},
             device_id_type=MESH,
         )
 
-    @pl.when(core == side)
-    def _():
-        sharing(me + 1 - 2 * core, 1 - core).start()
+    def transform(part):
+        acc[...] = jnp.zeros_like(acc)
+
+        @pl.loop(0, quarter)
+        def _(i):
+            for j in range(2):
+                source = i + j * quarter
+
+                @pl.when(source != seat)
+                def _():
+                    sending(part, source, source).wait_recv()
+
+            piece = jnp.concatenate([received[part, i], received[part, i + quarter]], axis=0)
+            acc[...] += jnp.dot(
+                piece,
+                table[pl.ds(pl.multiple_of(i * length, length), length), :],
+                preferred_element_type=jnp.float32,
+            )
+
+        picked = []
+        for g in range(spans):
+            piece = jnp.concatenate([received[part, g * per + t] for t in range(per)], axis=1)
+            picked.append(
+                jnp.dot(piece, pick[g], preferred_element_type=jnp.float32).astype(jnp.bfloat16)
+            )
+        ties = jnp.dot(
+            jnp.concatenate(picked, axis=1), put[...], preferred_element_type=jnp.float32
+        )
+        real, imag = turned(acc, rows, side)
+        for k in range(2 * WIDE // LANES):
+            at = k * LANES
+            source = real[:, at : at + LANES] if at < WIDE else imag[:, at - WIDE : at - WIDE + LANES]
+            whole[k] = source + ties[:, at : at + LANES]
+        for c in range(tile):
+            for k in range(2 * WIDE // LANES):
+                share[part, c, :, pl.ds(k * LANES, LANES)] = whole[
+                    k, pl.ds(c, segments, stride=tile), :
+                ]
+
+        @pl.when(core == side)
+        def _():
+            sharing(part, me + 1 - 2 * core, 1 - core).start()
+            for c in range(ch_local):
+                halves[part, side, c] = share[part, core * ch_local + c]
+
+        @pl.when(core != side)
+        def _():
+            sharing(part, across, 0).start()
+            sharing(part, across + 1, 1).start()
+
+    flags = flags_ref[...].astype(jnp.float32)
+    square = (segments, PARTS * segments)
+    diagonal = lax.broadcasted_iota(jnp.int32, square, 1) - lax.broadcasted_iota(
+        jnp.int32, square, 0
+    )
+
+    def whiten(part):
+        @pl.when(core != side)
+        def _():
+            arriving(part, side).wait_recv()
+
+        arriving(part, 1 - side).wait_recv()
         for c in range(ch_local):
-            halves[side, c] = share[core * ch_local + c]
-
-    @pl.when(core != side)
-    def _():
-        sharing(across, 0).start()
-        sharing(across + 1, 1).start()
-        arriving(side).wait_recv()
-
-    arriving(1 - side).wait_recv()
-
-    square = (segments, segments)
-    diagonal = lax.broadcasted_iota(jnp.int32, square, 0) == lax.broadcasted_iota(
-        jnp.int32, square, 1
-    )
-    flags = flags_ref[...].astype(jnp.float32)
-    flags = jnp.concatenate(
-        [
-            jnp.sum(jnp.where(diagonal, flags[c : c + 1, :], 0.0), axis=1, keepdims=True)
-            for c in range(ch_local)
-        ],
-        axis=0,
-    )
-    total = (halves[0] + halves[1]).reshape(ch_local * segments, 2 * WIDE)
-    real, imag = whiten_rows(total[:, :WIDE], total[:, WIDE:], flags)
-    own_rows = pl.ds(me * ch_local, ch_local)
-    everyone[own_rows, :, pl.ds(0, WIDE)] = real.reshape(ch_local, segments, WIDE)
-    everyone[own_rows, :, pl.ds(WIDE, WIDE)] = imag.reshape(ch_local, segments, WIDE)
+            total = halves[part, 0, c] + halves[part, 1, c]
+            picks = diagonal == part * segments
+            weight = jnp.sum(jnp.where(picks, flags[c : c + 1, :], 0.0), axis=1, keepdims=True)
+            real, imag = whiten_rows(total[:, :WIDE], total[:, WIDE:], weight)
+            everyone[part, me * ch_local + c, :, pl.ds(0, WIDE)] = real
+            everyone[part, me * ch_local + c, :, pl.ds(WIDE, WIDE)] = imag
 
     flip = {bit: me + bit - 2 * bit * (me // bit % 2) for bit in (1, 2, 4)}
 
-    def relay(source, h, target):
-        block = everyone.at[source * ch_local + h]
+    pairs = ch_local // PAIR
+
+    def relay(part, source, h, target):
+        block = everyone.at[part, pl.ds(source * ch_local + h * PAIR, PAIR)]
         return pltpu.make_async_remote_copy(
             src_ref=block,
             dst_ref=block,
             send_sem=relay_sem,
-            recv_sem=block_sem.at[source, h],
+            recv_sem=block_sem.at[part, source, h],
             device_id={"chan": target},
             device_id_type=MESH,
         )
 
-    def each_relay(zs, far, h, act):
+    def source_of(zs, far, h):
         first, second = ((4, 2), (2, 4))[h % 2]
         base = (me, flip[first], flip[second], flip[first] + flip[second] - me)[far]
-        source = base + (zs - z) * 8
+        return base + (zs - z) * 8
+
+    def each_relay(part, zs, far, h, act):
+        first, second = ((4, 2), (2, 4))[h % 2]
+        source = source_of(zs, far, h)
         if far == 0:
 
             @pl.when((zs <= z) & (z + 1 < depth))
             def _():
-                act(relay(source, h, me + 8))
+                act(relay(part, source, h, me + 8))
 
             @pl.when((zs >= z) & (z > 0))
             def _():
-                act(relay(source, h, me - 8))
-
-            act(relay(source, h, flip[first]))
+                act(relay(part, source, h, me - 8))
+
+            act(relay(part, source, h, flip[first]))
         if far <= 1:
-            act(relay(source, h, flip[second]))
-        act(relay(source, h, flip[1]))
-
-    def each_block(act):
-        @pl.loop(0, depth + 2)
+            act(relay(part, source, h, flip[second]))
+        act(relay(part, source, h, flip[1]))
+
+    def each_block(lowest, highest, act):
+        @pl.loop(lowest, highest)
         def _(wave):
             for far, hops in enumerate((0, 1, 1, 2)):
                 k = wave - hops
-                for side in (-1, 1):
-                    zs = z + side * k
+                for way in (-1, 1):
+                    zs = z + way * k
                     real_block = (k >= 0) & (k < depth) & (zs >= 0) & (zs < depth)
-                    if side == 1:
+                    if way == 1:
                         real_block = real_block & (k > 0)
 
                     @pl.when(real_block)
                     def _():
-                        for h in range(ch_local):
+                        for h in range(pairs):
                             act(zs, far, h)
 
-    def forward_block(zs, far, h):
-        first, second = ((4, 2), (2, 4))[h % 2]
-        base = (me, flip[first], flip[second], flip[first] + flip[second] - me)[far]
-        source = base + (zs - z) * 8
-
-        @pl.when(source != me)
-        def _():
-            relay(source, h, me).wait_recv()
-
-        each_relay(zs, far, h, lambda copy: copy.start())
-
-    each_block(forward_block)
-
-    @pl.loop(0, devices // 2)
-    def _(r):
-        source = 2 * r + flip[1] % 2
-        for h in range(ch_local):
-            relay(source, h, me).wait_recv()
+    def pass_on(part, lowest, highest):
+        def step(zs, far, h):
+            source = source_of(zs, far, h)
+
+            @pl.when(source != me)
+            def _():
+                relay(part, source, h, me).wait_recv()
+
+            each_relay(part, zs, far, h, lambda copy: copy.start())
+
+        each_block(lowest, highest, step)
+
+    transform(0)
+    whiten(0)
+    pass_on(0, 0, 1)
+    transform(1)
+    pass_on(0, 1, depth + 2)
+    whiten(1)
+    pass_on(1, 0, depth + 2)
+
+    for part in range(PARTS):
+
+        @pl.loop(0, devices // 2)
+        def _(r):
+            source = 2 * r + flip[1] % 2
+            for h in range(pairs):
+                relay(part, source, h, me).wait_recv()
+
+    for part in range(PARTS):
+        for c in range(ch_local):
+            at = pl.ds(part * segments, segments)
+            mine[c, at, :] = everyone[part, me * ch_local + c].astype(jnp.float32)
 
     group = 8
 
     @pl.loop(0, sources // group)
     def _(block):
         for s in range(group):
-            held[s] = everyone[ids_ref[block * group + s]].astype(jnp.float32)
+            for part in range(PARTS):
+                at = pl.ds(part * segments, segments)
+                held[s, at, :] = everyone[part, ids_ref[block * group + s]].astype(jnp.float32)
         lane = lax.broadcasted_iota(jnp.int32, (group, WIDE), 1)
         src_r, src_i = held[:, :, pl.ds(0, WIDE)], held[:, :, pl.ds(WIDE, WIDE)]
         for c in range(ch_local):
-            mine = everyone[me * ch_local + c].astype(jnp.float32)
-            rec_r, rec_i = mine[None, :, :WIDE], mine[None, :, WIDE:]
+            rec_r, rec_i = mine[c, :, pl.ds(0, WIDE)][None], mine[c, :, pl.ds(WIDE, WIDE)][None]
             real = jnp.sum(src_r * rec_r + src_i * rec_i, axis=1)
             imag = jnp.sum(src_i * rec_r - src_r * rec_i, axis=1)
             counts = jnp.sum(jnp.where(lane == BAND, real, 0.0), axis=1, keepdims=True)
@@ -440,30 +471,26 @@
         width = min(LAG_TILE, LAGS - first)
         out_ref[:, :, pl.ds(first, width)] = lags[:, :, :width]
 
-    for role in (1 - side, side):
-
-        @pl.loop(0, chips)
-        def _(k):
-            target = 2 * ((chip + k) % chips) + role
-
-            @pl.when(target != seat)
-            def _():
-                sending(target, seat).wait_send()
-
-    sharing(me + 1 - 2 * core, 1 - core).wait_send()
-
-    @pl.when(core != side)
-    def _():
-        sharing(across, 0).wait_send()
-
-    each_block(lambda zs, far, h: each_relay(zs, far, h, lambda copy: copy.wait_send()))
+    each_sending(lambda copy: copy.wait_send())
+    for part in range(PARTS):
+        sharing(part, me + 1 - 2 * core, 1 - core).wait_send()
+
+        @pl.when(core != side)
+        def _():
+            sharing(part, across, 0).wait_send()
+
+        each_block(
+            0,
+            depth + 2,
+            lambda zs, far, h: each_relay(part, zs, far, h, lambda copy: copy.wait_send()),
+        )
 
 
 def per_device(records, valid_flags, source_ids):
     devices = lax.axis_size("chan")
     segments, channels, length = records.shape
     ch_local = channels // devices
-    rows = ch_local * segments
+    short = segments // PARTS
     samples = length * devices
     sources = source_ids.shape[0]
     forward, inverse = forward_parts(samples), inverse_parts(samples)
@@ -477,26 +504,27 @@
         scratch_shapes=[
             pltpu.VMEM(forward.shape, jnp.float32),
             pltpu.VMEM(inverse.shape, jnp.float32),
-            pltpu.VMEM((devices // 2, segments, 2 * ch_local, length), jnp.bfloat16),
+            pltpu.VMEM((PARTS, devices // 2, short, 2 * ch_local, length), jnp.bfloat16),
             pltpu.VMEM((samples // 4, 2 * WIDE), jnp.bfloat16),
             pltpu.VMEM((2 * WIDE, LAGS_WIDE), jnp.bfloat16),
-            pltpu.VMEM((4 * rows, 2 * WIDE), jnp.float32),
+            pltpu.VMEM((4 * ch_local * short, 2 * WIDE), jnp.float32),
             pltpu.VMEM((SPANS // 2, samples // SPANS, SLOTS), jnp.bfloat16),
             pltpu.VMEM((SPANS // 2 * SLOTS, 2 * WIDE), jnp.bfloat16),
-            pltpu.VMEM((2 * WIDE // LANES, 2 * rows, LANES), jnp.float32),
-            pltpu.VMEM((2 * ch_local, segments, 2 * WIDE), jnp.float32),
-            pltpu.VMEM((2, ch_local, segments, 2 * WIDE), jnp.float32),
-            pltpu.VMEM((channels, segments, 2 * WIDE), jnp.bfloat16),
+            pltpu.VMEM((2 * WIDE // LANES, 2 * ch_local * short, LANES), jnp.float32),
+            pltpu.VMEM((PARTS, 2 * ch_local, short, 2 * WIDE), jnp.float32),
+            pltpu.VMEM((PARTS, 2, ch_local, short, 2 * WIDE), jnp.float32),
+            pltpu.VMEM((PARTS, channels, short, 2 * WIDE), jnp.bfloat16),
             pltpu.VMEM((8, segments, 2 * WIDE), jnp.float32),
+            pltpu.VMEM((ch_local, segments, 2 * WIDE), jnp.float32),
             pltpu.VMEM((2 * WIDE // LANES, ch_local * sources, LANES), jnp.float32),
             pltpu.SemaphoreType.DMA,
-            pltpu.SemaphoreType.DMA((devices // 2,)),
-            pltpu.SemaphoreType.DMA,
+            pltpu.SemaphoreType.DMA((PARTS, devices // 2)),
+            pltpu.SemaphoreType.DMA((PARTS,)),
             pltpu.SemaphoreType.DMA((2,)),
             pltpu.SemaphoreType.DMA,
-            pltpu.SemaphoreType.DMA((2,)),
+            pltpu.SemaphoreType.DMA((PARTS, 2)),
             pltpu.SemaphoreType.DMA,
-            pltpu.SemaphoreType.DMA((devices, ch_local)),
+            pltpu.SemaphoreType.DMA((PARTS, devices, ch_local // PAIR)),
         ],
         compiler_params=pltpu.CompilerParams(
             collective_id=0, has_side_effects=True, vmem_limit_bytes=56 << 20

time: 55.5 us -> 64.3 us (1.16)
  Pallas kernels: 53.1 us -> 61.9 us
    pallas_call x1, Pallas kernels: 53.1 us -> 61.9 us  [per_device(): pl.pallas_call(lambda *refs: kernel(devices, *refs), out_shape=jax.ShapeD...]
where the time goes in v2:
time: 64.3 us; the launch traced here: 64.2 us
  Pallas kernels  61.9 us (96%)
  local copies, waits for them, and re-layouts  2.26 us (4%)
    pallas_call x1, Pallas kernels, per_device(): pl.pallas_call(lambda *refs: kernel(devices, *refs), out_shape=jax.ShapeD...  61.9 us
    unnamed x1, local copies, waits for them, and re-layouts  2.26 us

profile of v2, /device:TPU:1, one launch (start us, length us, event | category | flops | bytes accessed | tf_op | source)
XLA Modules:
  0.0 64.2 jit_solution(17743619860003180344)
XLA Ops:
  0.0 61.9 %correlate.1 = f32[64,4,1001]{2,1,0:T(4,128)} custom-call(s32[64]{0:T(128)} %refs_0_.1, s32[4,8]{1,0:T(4,128)} %bitcast.1, bf16[8,128,512]{2,1,0:T(8,128)(2,1)} %refs_2_.1, f32[400,640]{1,0:T(8,128)} %constant.4.clone.refs_3_, f32[160,1024]{1,0:T(8,128)} %constant.5.clone.refs_4_), custom_call_target="tpu_custom_call" | custom-call | tf_op jit(solution)/shard_map/correlate/pallas_call | solution.py:499
  61.9 2.3 %copy.7 = f32[64,4,1001]{2,1,0:T(4,128)} copy(f32[64,4,1001]{2,1,0:T(4,128)} %correlate.1) | data formatting | bytes 2050048
